TPU v7x, 128 devices: a whole 4x4x4 slice. The times are simulated.
128 devices in a mesh: sample: 8 (over x, core), gene: 4 (over y), cohort: 4 (over z).
Axes of the slice: x: 4, y: 4, z: 4, core: 2. Of those that a mesh axis runs over, the one named last changes fastest.
Arguments:
- dosage: bfloat16 [16384, 32768], P(('sample', 'cohort'), 'gene'), may hold values from 0 to 2
- covariates: bfloat16 [16384, 32], P(('sample', 'cohort')), may hold values from 0 to 2
- phenotype: bfloat16 [16384], P(('sample', 'cohort')), may hold values from -6 to 6
- sample_mask: int32 [16384], P(('sample', 'cohort')), may hold values 0 or 1
- variant_weight: float32 [32768], replicated, may hold values from 0.1 to 1
- bucket_owner: int32 [256], replicated, may hold values from 0 to 15, as said below
- variant_gene: int32 [32768], replicated, may hold values from -1 to 127, as said below
Outputs:
- gram_tiles: float32 [16, 16, 128, 128], P(('gene', 'cohort'), 'sample')
- rho_stats: float32 [8, 128], P(None, ('gene', 'cohort'))
- gene_trace: float32 [128], P(('gene', 'cohort'))
Inputs may be any that keep to these rules, and one draw needn't show every extreme that they name: `bucket_owner`: every owner holds exactly 16 buckets, at most 8 of them among the 64 buckets of one index of gene, and some owner exactly 8; of the buckets of one index of gene, exactly 16 belong to owners whose index leaves a given remainder on division by the size of the cohort axis. `variant_gene`: genes o * 8 to (o + 1) * 8 - 1 lie in the buckets of owner o, each in one or more whole buckets that are consecutive among that owner's buckets; all its buckets are full but its last, whose first 10 to 128 columns are live and the rest -1.
All inputs are finite; a program needn't handle non-finite values. No bound on the sum of `sample_mask` on one device may be relied on, other than what follows from the above.
Results may differ from a plain program's by a relative error of at most 0.0003.
Values may be sent and summed in bfloat16 or wider, within the bound.
No kernel may reach another device: no remote copies, remote signals or barrier semaphores. Data moves between devices by JAX's collectives and lax.ppermute only.
A program may use at most 128 MiB of HBM per device.

v0:
```python
import math
import jax
import jax.numpy as jnp
from jax import lax
from jax.sharding import PartitionSpec as P

BUCKET_WIDTH = 128
GENES_OWN = 8
RHO_GRID = (0.0, 0.01, 0.04, 0.09, 0.16, 0.25, 0.5, 1.0)


def solve_moments(factor, rhs):
    half = lax.linalg.triangular_solve(factor, rhs, left_side=True, lower=True)
    return lax.linalg.triangular_solve(factor, half, left_side=True, lower=True, transpose_a=True)


def inner_rows(first, second):
    return lax.dot_general(
        first, second, (((0,), (0,)), ((), ())), preferred_element_type=jnp.float32
    )


def block_rank(labels, group_count, label_count):
    onehot = (labels[:, None] == jnp.arange(label_count, dtype=jnp.int32)[None, :]).astype(
        jnp.int32
    )
    blocks = onehot.reshape(group_count, labels.shape[0] // group_count, label_count)
    return jnp.sum((jnp.cumsum(blocks, axis=1) - blocks) * blocks, axis=2).reshape(labels.shape[0])


def finish_slots(
    gram, cross, slot_bucket, moments, variant_weight, variant_gene, owner_here, sample_total
):
    cov_count = moments.shape[0]
    slot_count = gram.shape[0]
    span_width = gram.shape[1]
    factor = jnp.linalg.cholesky(moments[:, :cov_count])
    beta_hat = solve_moments(factor, moments[:, cov_count:])[:, 0]
    cov_cross = cross[:, :cov_count, :]
    raw_score = cross[:, cov_count, :]
    stacked = jnp.transpose(cov_cross, (1, 0, 2)).reshape(cov_count, slot_count * span_width)
    solved = solve_moments(factor, stacked).reshape(cov_count, slot_count, span_width)
    projected = jnp.einsum("bcj,cbk->bjk", cov_cross, solved, precision=lax.Precision.HIGHEST)
    scores = raw_score - jnp.einsum(
        "bcj,c->bj", cov_cross, beta_hat, precision=lax.Precision.HIGHEST
    )
    bucket_total = variant_gene.shape[0] // span_width
    weight_rows = jnp.where(variant_gene >= 0, variant_weight, 0.0).reshape(
        bucket_total, span_width
    )
    live_weight = jnp.take(weight_rows, slot_bucket, axis=0)
    tiles = live_weight[:, :, None] * live_weight[:, None, :] * (gram - projected) / sample_total
    zscore = (live_weight * scores / math.sqrt(sample_total)).reshape(slot_count * span_width)
    gene_rows = (
        jnp.take(variant_gene.reshape(bucket_total, span_width), slot_bucket, axis=0)
        - owner_here * GENES_OWN
    )
    member = (
        gene_rows.reshape(slot_count * span_width)[:, None]
        == jnp.arange(GENES_OWN, dtype=jnp.int32)[None, :]
    ).astype(jnp.float32)
    squares = jnp.dot(zscore * zscore, member, precision=lax.Precision.HIGHEST)
    burden_sum = jnp.dot(zscore, member, precision=lax.Precision.HIGHEST)
    diagonal = jnp.diagonal(tiles, axis1=1, axis2=2).reshape(slot_count * span_width)
    trace_sum = jnp.dot(diagonal, member, precision=lax.Precision.HIGHEST)
    return (tiles, squares, burden_sum, trace_sum)


def shards(dosage, covariates, phenotype, sample_mask, variant_weight, bucket_owner, variant_gene):
    gene_count = lax.axis_size("gene")
    cohort_count = lax.axis_size("cohort")
    sample_count = lax.axis_size("sample")
    owner_count = gene_count * cohort_count
    span_width = BUCKET_WIDTH
    sample_rows = dosage.shape[0]
    src_buckets = dosage.shape[1] // span_width
    total_buckets = bucket_owner.shape[0]
    held_slots = total_buckets // owner_count
    cap_slots = held_slots // 2
    share = held_slots // sample_count
    sample_total = sample_rows * sample_count * cohort_count
    cohort_here = lax.axis_index("cohort")
    owner_here = lax.axis_index("gene") * cohort_count + cohort_here
    sample_keep = sample_mask.astype(jnp.bfloat16)
    masked_cov = covariates * sample_keep[:, None]
    left_cols = jnp.concatenate([masked_cov, (phenotype * sample_keep)[:, None]], axis=1)
    moments = lax.psum(
        inner_rows(masked_cov, jnp.concatenate([covariates, phenotype[:, None]], axis=1)),
        ("sample", "cohort"),
    )
    masked_dosage = (dosage * sample_keep[:, None]).reshape(sample_rows, src_buckets, span_width)
    owner_ids = jnp.arange(owner_count, dtype=jnp.int32)
    onehot = (bucket_owner[:, None] == owner_ids[None, :]).astype(jnp.int32)
    owner_rank = jnp.sum((jnp.cumsum(onehot, axis=0) - onehot) * onehot, axis=1)
    pair_rank = block_rank(bucket_owner, gene_count, owner_count)
    source_start = lax.axis_index("gene") * src_buckets
    mine_owner = lax.dynamic_slice_in_dim(bucket_owner, source_start, src_buckets)
    mine_rank = lax.dynamic_slice_in_dim(pair_rank, source_start, src_buckets)
    own_key = jnp.where(bucket_owner == owner_here, owner_rank, held_slots)
    own_bucket = (
        jnp.zeros((held_slots,), jnp.int32)
        .at[own_key]
        .set(jnp.arange(total_buckets, dtype=jnp.int32), mode="drop")
    )
    own_source = own_bucket // src_buckets
    own_pair = jnp.take(pair_rank, own_bucket)
    cohort_ids = jnp.arange(cohort_count, dtype=jnp.int32)
    flat_index = (
        (own_source[None, :] * cohort_count + cohort_ids[:, None]) * cap_slots + own_pair[None, :]
    ).reshape(cohort_count * held_slots)
    send_from = (
        jnp.full((owner_count * cap_slots,), -1, jnp.int32)
        .at[mine_owner * cap_slots + mine_rank]
        .set(jnp.arange(src_buckets, dtype=jnp.int32))
    )
    send_pick = jnp.maximum(send_from, 0)
    cohort_left = lax.all_gather(left_cols[:, None, :], "cohort", axis=1, tiled=True)
    packed = (
        jnp.take(masked_dosage, send_pick, axis=1)
        * (send_from >= 0).astype(jnp.bfloat16)[None, :, None]
    )
    packed = packed.reshape(sample_rows, owner_count, cap_slots, span_width)
    arrived = lax.all_to_all(packed, ("gene", "cohort"), split_axis=1, concat_axis=1, tiled=True)
    arrived = arrived.reshape(sample_rows, owner_count * cap_slots, span_width)
    owned = jnp.take(arrived, flat_index, axis=1).reshape(
        sample_rows, cohort_count, held_slots, span_width
    )
    gram = jnp.einsum("schj,schk->hjk", owned, owned, preferred_element_type=jnp.float32)
    cross = jnp.einsum("sci,schk->hik", cohort_left, owned, preferred_element_type=jnp.float32)
    slot_start = lax.axis_index("sample") * share
    gram, cross = lax.psum((gram, cross), "sample")
    tiles, squares, burden_sum, trace_sum = finish_slots(
        gram, cross, own_bucket, moments, variant_weight, variant_gene, owner_here, sample_total
    )
    tiles = lax.dynamic_slice_in_dim(tiles, slot_start, share)
    rho_col = jnp.array(RHO_GRID, dtype=jnp.float32)[:, None]
    rho_stats = (
        (1.0 - rho_col) * squares[None, :] + rho_col * (burden_sum * burden_sum)[None, :]
    ) / span_width
    gene_trace = trace_sum / span_width
    return (tiles[None], rho_stats, gene_trace)


def solution(mesh):
    placed = (
        P(("sample", "cohort"), "gene"),
        P(("sample", "cohort"), None),
        P(("sample", "cohort")),
        P(("sample", "cohort")),
        P(),
        P(),
        P(),
    )
    return jax.shard_map(
        shards,
        mesh=mesh,
        in_specs=placed,
        out_specs=(
            P(("gene", "cohort"), "sample", None, None),
            P(None, ("gene", "cohort")),
            P(("gene", "cohort")),
        ),
        check_vma=False,
    )
```

profile of v0, /device:TPU:0, one launch (start us, length us, event | category | flops | bytes accessed | tf_op | source)
XLA Modules:
  0.0 636.7 jit_solution(13550545437215399836)
XLA Ops:
  7.2 0.8 eq.67
  7.9 0.1 fusion.23
  8.0 0.1 reduce_window_sum.28
  8.2 0.2 select_reduce_fusion
  8.5 0.8 compare_select_fusion.3
  9.3 0.8 scatter_custom_fusion.1
  10.1 12.0 %copy.54 = bf16[512,8192]{0,1:T(8,128)(2,1)} copy(bf16[512,8192]{1,0:T(8,128)(2,1)} %param.8) | data formatting | bytes 16777216 | tf_op args[0]
  22.1 7.1 %broadcast_multiply_fusion = bf16[512,8192]{0,1:T(8,128)(2,1)} fusion(bf16[512,8192]{0,1:T(8,128)(2,1)} %copy.54, bf16[512]{0:T(512)(128)(2,1)S(1)} %get-tuple-element.9), kind=kLoop, calls=%fused_computation.14 | loop fusion | flops 4194304 | bytes 16778240 | tf_op jit(solution)/shard_map/mul | solution.py:91
  29.2 11.9 %copy.55 = bf16[512,64,128]{2,0,1:T(8,128)(2,1)} copy(bf16[512,64,128]{0,2,1:T(8,128)(2,1)} %bitcast.130) | data formatting | bytes 16777216 | tf_op jit(solution)/shard_map/reshape | solution.py:91
  41.1 0.1 reshape.226
  41.2 0.1 broadcast_in_dim.106
  41.3 11.5 %gather_fusion.2 = bf16[128,512,128]{2,1,0:T(8,128)(2,1)} fusion(bf16[512,64,128]{2,0,1:T(8,128)(2,1)} %copy.55, s32[1024]{0:T(1024)S(1)} %pad_clamp_fusion.1), kind=kCustom, calls=%fused_computation.2 | custom fusion | bytes 33554944 | tf_op jit(solution)/shard_map/jit(_take)/gather | solution.py:119
  52.8 14.2 %select_multiply_fusion = bf16[512,16,8,128]{3,0,2,1:T(8,128)(2,1)} fusion(bf16[512,16,8,128]{3,0,2,1:T(8,128)(2,1)} %bitcast.127, pred[16,8]{1,0:T(8,128)(4,1)S(1)} %broadcast_in_dim.106, bf16[16,8]{1,0:T(8,128)(2,1)S(1)} %reshape.226), kind=kLoop, calls=%fused_computation.8 | loop fusion | flops 16777216 | bytes 33554816 | tf_op jit(solution)/shard_map/mul | solution.py:119
  67.0 8.3 %all-to-all-start = ((bf16[512,16,8,128]{3,0,2,1:T(8,128)(2,1)}), bf16[512,16,8,128]{3,0,2,1:T(8,128)(2,1)}, u32[]{:S(2)}, u32[]{:S(2)}) async-start(bf16[512,16,8,128]{3,0,2,1:T(8,128)(2,1)} %select_multiply_fusion), calls=%async_computation | async-start | bytes 33554432 | tf_op jit(solution)/shard_map/all_to_all | solution.py:123
  75.5 0.6 reduce-window.6
  76.1 0.2 slice_reduce_fusion
  76.3 0.1 fusion.31
  76.4 1.4 scatter_custom_fusion
  77.8 0.7 gather_fusion.1
  78.6 160.0 %all-gather.1 = bf16[4,33,512]{2,1,0:T(8,128)(2,1)S(1)} all-gather(bf16[1,33,512]{2,1,0:T(8,128)(2,1)S(1)} %maximum_bitcast_fusion), channel_id=2, replica_groups=mesh['sample'=8,'gene'=4,'cohort'=4] {'cohort'}, dimensions={0}, use_global_device_ids=true | all-gather | bytes 168960 | tf_op jit(solution)/shard_map/all_gather | solution.py:117
  238.8 0.1 fusion.24
  238.9 197.3 %psum.23 = f32[32,33]{0,1:T(8,128)S(1)} all-reduce(f32[32,33]{0,1:T(8,128)S(1)} %fusion.24), channel_id=1, replica_groups=mesh['sample'=8,'gene'=4,'cohort'=4] {'sample','cohort'}, use_global_device_ids=true, to_apply=%region_9.10 | all-reduce | flops 1056 | bytes 8448 | tf_op jit(solution)/shard_map/psum | solution.py:87
  436.3 2.9 cholesky.16
  439.2 0.6 compare_reduce_fusion
  439.9 0.7 fusion.28
  440.5 2.4 custom-call.12
  443.0 0.6 gather_fusion
  443.6 0.6 gather_fusion.4
  444.2 11.7 %gather_fusion.3 = bf16[64,512,128]{2,1,0:T(8,128)(2,1)} fusion(bf16[512,128,128]{2,0,1:T(8,128)(2,1)} %bitcast.6, s32[1024]{0:T(1024)S(1)} %pad_clamp_fusion), kind=kCustom, calls=%fused_computation.3 | custom fusion | bytes 16777472 | tf_op jit(solution)/shard_map/jit(_take)/gather | solution.py:125
  456.0 12.0 %copy.56 = bf16[512,64,128]{2,1,0:T(8,128)(2,1)} copy(bf16[512,64,128]{2,0,1:T(8,128)(2,1)} %bitcast.128) | data formatting | bytes 16777216 | tf_op jit(solution)/shard_map/jit(_take)/gather | solution.py:125
  467.9 7.4 %broadcast_select_fusion = bf16[512,4,16,128]{3,2,1,0:T(8,128)(2,1)} fusion(bf16[512,4,16,128]{3,2,1,0:T(8,128)(2,1)} %bitcast.129, pred[4,16]{1,0:T(4,128)(4,1)S(1)} %compare_and_fusion), kind=kLoop, calls=%fused_computation.9 | loop fusion | flops 4194304 | bytes 16777280 | tf_op jit(solution)/shard_map/jit(_take)/select_n | solution.py:125
  475.3 25.9 %fusion.4 = f32[16,128,128]{2,1,0:T(8,128)} fusion(bf16[512,4,16,128]{3,2,1,0:T(8,128)(2,1)} %broadcast_select_fusion), kind=kOutput, calls=%fused_computation.15 | convolution fusion | flops 1073741824 | bytes 9437184 | tf_op jit(solution)/shard_map/schj,schk->hjk/dot_general | solution.py:128
  501.2 8.8 %fusion.9 = f32[16,33,128]{2,1,0:T(8,128)} fusion(bf16[512,4,33,1]{0,2,1,3:T(8,128)(2,1)S(1)} %reshape.299, bf16[512,4,16,128]{3,2,1,0:T(8,128)(2,1)} %broadcast_select_fusion), kind=kOutput, calls=%fused_computation.19 | convolution fusion | flops 276824064 | bytes 8794112 | tf_op jit(solution)/shard_map/sci,schk->hik/dot_general | solution.py:129
  510.0 0.1 convolution_bitcast_fusion.1
  510.2 0.1 convolution_bitcast_fusion
  510.4 101.9 %all-reduce.3.cloned.1.call-done = (f32[16,128,128]{2,1,0:T(8,128)}, f32[16,33,128]{2,1,0:T(8,128)}) async-done(((f32[16,128,128]{2,1,0:T(8,128)}, f32[16,33,128]{2,1,0:T(8,128)}), (f32[16,128,128]{2,1,0:T(8,128)}, f32[16,33,128]{2,1,0:T(8,128)})) %all-reduce.3.cloned.1.call-update) | async-done | bytes 1318928 | tf_op jit(solution)/shard_map/psum | solution.py:131
  612.3 0.8 slice.59
  613.1 1.4 fusion.17
  614.5 1.2 fusion.20
  615.7 0.4 fusion.33
  616.2 3.3 fusion.8
  619.5 4.6 copy.65
  624.1 1.8 gather_fusion.5
  626.0 1.1 fusion.12
  627.1 0.6 convolution_bitcast_fusion.4
  627.7 0.6 fusion.13
  628.3 0.7 dynamic-slice_bitcast_fusion
  628.9 0.7 add_multiply_fusion
  (53 shorter events, 0.9 us)
Async XLA Ops:
  10.1 12.0 %copy-start.4 = (bf16[512]{0:T(512)(128)(2,1)S(1)}, bf16[512]{0:T(512)(128)(2,1)}, u32[]{:S(2)}) copy-start(bf16[512]{0:T(512)(128)(2,1)} %param.10) | copy-start | bytes 3076
  10.1 12.0 %copy-start.5 = (s32[512]{0:T(512)S(1)}, s32[512]{0:T(512)}, u32[]{:S(2)}) copy-start(s32[512]{0:T(512)} %param.11) | copy-start | bytes 6148
  67.0 8.4 %copy-start.3 = (s32[256]{0:T(256)S(1)}, s32[256]{0:T(256)}, u32[]{:S(2)}) copy-start(s32[256]{0:T(256)} %param.13) | copy-start | bytes 3076
  67.0 11.6 %copy-start.2 = (bf16[512,32]{0,1:T(8,128)(2,1)S(1)}, bf16[512,32]{0,1:T(8,128)(2,1)}, u32[]{:S(2)}) copy-start(bf16[512,32]{0,1:T(8,128)(2,1)} %param.9) | copy-start | bytes 98308
  67.0 375.9 %copy-start = (s32[32768]{0:T(1024)S(1)}, s32[32768]{0:T(1024)}, u32[]{:S(2)}) copy-start(s32[32768]{0:T(1024)} %param.14) | copy-start | bytes 393220
  67.0 375.9 %copy-start.1 = (f32[32768]{0:T(1024)S(1)}, f32[32768]{0:T(1024)}, u32[]{:S(2)}) copy-start(f32[32768]{0:T(1024)} %param.12) | copy-start | bytes 393220
  67.0 377.2 %all-to-all-start = ((bf16[512,16,8,128]{3,0,2,1:T(8,128)(2,1)}), bf16[512,16,8,128]{3,0,2,1:T(8,128)(2,1)}, u32[]{:S(2)}, u32[]{:S(2)}) async-start(bf16[512,16,8,128]{3,0,2,1:T(8,128)(2,1)} %select_multiply_fusion), calls=%async_computation | async-start | bytes 33554432 | tf_op jit(solution)/shard_map/all_to_all | solution.py:123
  75.4 536.9 %all-reduce.3.cloned.1.call-start = ((), (), s32[]{:S(2)}) async-start(), calls=%async_computation.1 | async-start | bytes 2752512 | tf_op jit(solution)/shard_map/psum | solution.py:131
  510.0 119.0 %copy-start.6 = (f32[8]{0:T(128)S(1)}, f32[8]{0:T(128)}, u32[]{:S(2)}) copy-start(f32[8]{0:T(128)} %constant.200.clone) | copy-start | bytes 100
  510.0 119.0 %copy-start.7 = (f32[8]{0:T(128)S(1)}, f32[8]{0:T(128)}, u32[]{:S(2)}) copy-start(f32[8]{0:T(128)} %constant.202) | copy-start | bytes 100
Sparse Core Ops, SparseCore 0:
  510.1 102.1 all-reduce.2
where the time goes:
time: 643 us; the launch traced here: 637 us
  blocking collectives  357 us (56%)
  waiting for transfers between devices  102 us (16%)
  local copies, waits for them, and re-layouts  72.6 us (11%)
  matrix products  43.6 us (7%)
  other arithmetic  38.3 us (6%)
  between operations  14.6 us (2%)
  starting transfers between devices  8.38 us (1%)
    psum x1, blocking collectives, shards(): lax.psum(inner_rows(masked_cov, jnp.concatenate([covariates, phenotype[:,...  197 us
    all_gather x1, blocking collectives, shards(): lax.all_gather(left_cols[:, None, :], 'cohort', axis=1, tiled=True)  160 us
    psum x1, waiting for transfers between devices, shards(): gram, cross = lax.psum((gram, cross), 'sample')  102 us
    dot_general x1, matrix products, shards(): jnp.einsum('schj,schk->hjk', owned, owned, preferred_element_type=jnp.flo...  25.9 us
    gather x2, local copies, waits for them, and re-layouts, shards(): jnp.take(arrived, flat_index, axis=1)  23.7 us
    mul x2, other arithmetic, shards(): jnp.take(masked_dosage, send_pick, axis=1)  14.2 us
  transfers between devices with their start and end apart: 2, of which 1 were waited for; matrix products, arithmetic and copies ran while one was open for 2% of the time, Pallas kernels for 0%

commit v1 on v0

--- a/solution.py
+++ b/solution.py
@@ -85,8 +85,11 @@
     masked_cov = covariates * sample_keep[:, None]
     left_cols = jnp.concatenate([masked_cov, (phenotype * sample_keep)[:, None]], axis=1)
     moments = lax.psum(
-        inner_rows(masked_cov, jnp.concatenate([covariates, phenotype[:, None]], axis=1)),
-        ("sample", "cohort"),
+        lax.psum(
+            inner_rows(masked_cov, jnp.concatenate([covariates, phenotype[:, None]], axis=1)),
+            "cohort",
+        ),
+        "sample",
     )
     masked_dosage = (dosage * sample_keep[:, None]).reshape(sample_rows, src_buckets, span_width)
     owner_ids = jnp.arange(owner_count, dtype=jnp.int32)

time: 643 us -> 535 us (0.83)
  blocking collectives: 357 us -> 251 us
    psum x1, blocking collectives: 197 us -> 66.5 us  [shards(): lax.psum(inner_rows(masked_cov, jnp.concatenate([covariates, phenotype[:,...]
    psum x1, waiting for transfers between devices: 102 us -> 68.6 us  [shards(): gram, cross = lax.psum((gram, cross), 'sample')]
    all_to_all x1, waiting for transfers between devices: 0.01 us -> 30.6 us  [shards(): lax.all_to_all(packed, ('gene', 'cohort'), split_axis=1, concat_axis=1, t...]
    psum x0 -> x1, blocking collectives: none -> 24.8 us  [shards(): lax.psum(lax.psum(inner_rows(masked_cov, jnp.concatenate([covariates, phe...]
  transfers between devices with their start and end apart: 2 -> 2, of which waited for: 1 -> 2; matrix products, arithmetic and copies ran while one was open for 2% -> 2% of each run, Pallas kernels for 0% -> 0%
where the time goes in v1:
time: 535 us; the launch traced here: 528 us
  blocking collectives  251 us (47%)
  waiting for transfers between devices  99.2 us (19%)
  local copies, waits for them, and re-layouts  72.6 us (14%)
  matrix products  43.6 us (8%)
  other arithmetic  38.3 us (7%)
  between operations  14.6 us (3%)
  starting transfers between devices  8.38 us (2%)
    all_gather x1, blocking collectives, shards(): lax.all_gather(left_cols[:, None, :], 'cohort', axis=1, tiled=True)  160 us
    psum x1, waiting for transfers between devices, shards(): gram, cross = lax.psum((gram, cross), 'sample')  68.6 us
    psum x1, blocking collectives, shards(): lax.psum(inner_rows(masked_cov, jnp.concatenate([covariates, phenotype[:,...  66.5 us
    all_to_all x1, waiting for transfers between devices, shards(): lax.all_to_all(packed, ('gene', 'cohort'), split_axis=1, concat_axis=1, t...  30.6 us
    dot_general x1, matrix products, shards(): jnp.einsum('schj,schk->hjk', owned, owned, preferred_element_type=jnp.flo...  25.9 us
    psum x1, blocking collectives, shards(): lax.psum(lax.psum(inner_rows(masked_cov, jnp.concatenate([covariates, phe...  24.8 us
    gather x2, local copies, waits for them, and re-layouts, shards(): jnp.take(arrived, flat_index, axis=1)  23.7 us
    mul x2, other arithmetic, shards(): jnp.take(masked_dosage, send_pick, axis=1)  14.2 us
  transfers between devices with their start and end apart: 2, of which 2 were waited for; matrix products, arithmetic and copies ran while one was open for 2% of the time, Pallas kernels for 0%

profile of v1, /device:TPU:0, one launch (start us, length us, event | category | flops | bytes accessed | tf_op | source)
XLA Modules:
  0.0 527.9 jit_solution(8980923891999409403)
XLA Ops:
  7.2 0.8 eq.67
  7.9 0.1 fusion.23
  8.0 0.1 reduce_window_sum.28
  8.2 0.2 select_reduce_fusion
  8.5 0.8 compare_select_fusion.3
  9.3 0.8 scatter_custom_fusion.1
  10.1 12.0 %copy.54 = bf16[512,8192]{0,1:T(8,128)(2,1)} copy(bf16[512,8192]{1,0:T(8,128)(2,1)} %param.8) | data formatting | bytes 16777216 | tf_op args[0]
  22.1 7.1 %broadcast_multiply_fusion = bf16[512,8192]{0,1:T(8,128)(2,1)} fusion(bf16[512,8192]{0,1:T(8,128)(2,1)} %copy.54, bf16[512]{0:T(512)(128)(2,1)S(1)} %get-tuple-element.9), kind=kLoop, calls=%fused_computation.14 | loop fusion | flops 4194304 | bytes 16778240 | tf_op jit(solution)/shard_map/mul | solution.py:94
  29.2 11.9 %copy.55 = bf16[512,64,128]{2,0,1:T(8,128)(2,1)} copy(bf16[512,64,128]{0,2,1:T(8,128)(2,1)} %bitcast.130) | data formatting | bytes 16777216 | tf_op jit(solution)/shard_map/reshape | solution.py:94
  41.2 0.1 broadcast_in_dim.106
  41.3 11.5 %gather_fusion.2 = bf16[128,512,128]{2,1,0:T(8,128)(2,1)} fusion(bf16[512,64,128]{2,0,1:T(8,128)(2,1)} %copy.55, s32[1024]{0:T(1024)S(1)} %pad_clamp_fusion.1), kind=kCustom, calls=%fused_computation.2 | custom fusion | bytes 33554944 | tf_op jit(solution)/shard_map/jit(_take)/gather | solution.py:122
  52.8 14.2 %select_multiply_fusion = bf16[512,16,8,128]{3,0,2,1:T(8,128)(2,1)} fusion(bf16[512,16,8,128]{3,0,2,1:T(8,128)(2,1)} %bitcast.127, pred[16,8]{1,0:T(8,128)(4,1)S(1)} %broadcast_in_dim.106, bf16[16,8]{1,0:T(8,128)(2,1)S(1)} %reshape.226), kind=kLoop, calls=%fused_computation.8 | loop fusion | flops 16777216 | bytes 33554816 | tf_op jit(solution)/shard_map/mul | solution.py:122
  67.0 8.3 %all-to-all-start = ((bf16[512,16,8,128]{3,0,2,1:T(8,128)(2,1)}), bf16[512,16,8,128]{3,0,2,1:T(8,128)(2,1)}, u32[]{:S(2)}, u32[]{:S(2)}) async-start(bf16[512,16,8,128]{3,0,2,1:T(8,128)(2,1)} %select_multiply_fusion), calls=%async_computation | async-start | bytes 33554432 | tf_op jit(solution)/shard_map/all_to_all | solution.py:126
  75.5 0.6 reduce-window.6
  76.1 0.2 slice_reduce_fusion
  76.4 1.4 scatter_custom_fusion
  77.8 0.7 gather_fusion.1
  78.6 160.0 %all-gather.1 = bf16[4,33,512]{2,1,0:T(8,128)(2,1)S(1)} all-gather(bf16[1,33,512]{2,1,0:T(8,128)(2,1)S(1)} %maximum_bitcast_fusion), channel_id=2, replica_groups=mesh['sample'=8,'gene'=4,'cohort'=4] {'cohort'}, dimensions={0}, use_global_device_ids=true | all-gather | bytes 168960 | tf_op jit(solution)/shard_map/all_gather | solution.py:120
  238.8 0.1 fusion.24
  238.9 66.5 %psum.30 = f32[32,33]{0,1:T(8,128)S(1)} all-reduce(f32[32,33]{0,1:T(8,128)S(1)} %fusion.24), channel_id=1, replica_groups=mesh['sample'=8,'gene'=4,'cohort'=4] {'cohort'}, use_global_device_ids=true, to_apply=%region_9.10 | all-reduce | flops 1056 | bytes 8448 | tf_op jit(solution)/shard_map/psum | solution.py:88
  305.4 24.8 %psum.31 = f32[32,33]{0,1:T(8,128)S(1)} all-reduce(f32[32,33]{0,1:T(8,128)S(1)} %psum.30), channel_id=1, replica_groups=mesh['sample'=8,'gene'=4,'cohort'=4] {'sample'}, use_global_device_ids=true, to_apply=%region_10.11 | all-reduce | flops 1056 | bytes 8448 | tf_op jit(solution)/shard_map/psum | solution.py:87
  330.3 2.9 cholesky.16
  333.2 0.6 compare_reduce_fusion
  333.9 0.7 fusion.28
  334.5 2.4 custom-call.12
  337.0 0.6 gather_fusion
  337.6 0.6 gather_fusion.4
  338.2 30.6 %all-to-all-done = bf16[512,16,8,128]{3,0,2,1:T(8,128)(2,1)} async-done(((bf16[512,16,8,128]{3,0,2,1:T(8,128)(2,1)}), bf16[512,16,8,128]{3,0,2,1:T(8,128)(2,1)}, u32[]{:S(2)}, u32[]{:S(2)}) %all-to-all-start) | async-done | bytes 16777248 | tf_op jit(solution)/shard_map/all_to_all | solution.py:126
  368.8 11.7 %gather_fusion.3 = bf16[64,512,128]{2,1,0:T(8,128)(2,1)} fusion(bf16[512,128,128]{2,0,1:T(8,128)(2,1)} %bitcast.6, s32[1024]{0:T(1024)S(1)} %pad_clamp_fusion), kind=kCustom, calls=%fused_computation.3 | custom fusion | bytes 16777472 | tf_op jit(solution)/shard_map/jit(_take)/gather | solution.py:128
  380.5 12.0 %copy.56 = bf16[512,64,128]{2,1,0:T(8,128)(2,1)} copy(bf16[512,64,128]{2,0,1:T(8,128)(2,1)} %bitcast.128) | data formatting | bytes 16777216 | tf_op jit(solution)/shard_map/jit(_take)/gather | solution.py:128
  392.5 7.4 %broadcast_select_fusion = bf16[512,4,16,128]{3,2,1,0:T(8,128)(2,1)} fusion(bf16[512,4,16,128]{3,2,1,0:T(8,128)(2,1)} %bitcast.129, pred[4,16]{1,0:T(4,128)(4,1)S(1)} %compare_and_fusion), kind=kLoop, calls=%fused_computation.9 | loop fusion | flops 4194304 | bytes 16777280 | tf_op jit(solution)/shard_map/jit(_take)/select_n | solution.py:128
  399.9 25.9 %fusion.4 = f32[16,128,128]{2,1,0:T(8,128)} fusion(bf16[512,4,16,128]{3,2,1,0:T(8,128)(2,1)} %broadcast_select_fusion), kind=kOutput, calls=%fused_computation.15 | convolution fusion | flops 1073741824 | bytes 9437184 | tf_op jit(solution)/shard_map/schj,schk->hjk/dot_general | solution.py:131
  425.8 8.8 %fusion.9 = f32[16,33,128]{2,1,0:T(8,128)} fusion(bf16[512,4,33,1]{0,2,1,3:T(8,128)(2,1)S(1)} %reshape.299, bf16[512,4,16,128]{3,2,1,0:T(8,128)(2,1)} %broadcast_select_fusion), kind=kOutput, calls=%fused_computation.19 | convolution fusion | flops 276824064 | bytes 8794112 | tf_op jit(solution)/shard_map/sci,schk->hik/dot_general | solution.py:132
  434.6 0.1 convolution_bitcast_fusion.1
  434.7 0.1 convolution_bitcast_fusion
  434.9 68.6 %all-reduce.3.cloned.1.call-done = (f32[16,128,128]{2,1,0:T(8,128)}, f32[16,33,128]{2,1,0:T(8,128)}) async-done(((f32[16,128,128]{2,1,0:T(8,128)}, f32[16,33,128]{2,1,0:T(8,128)}), (f32[16,128,128]{2,1,0:T(8,128)}, f32[16,33,128]{2,1,0:T(8,128)})) %all-reduce.3.cloned.1.call-update) | async-done | bytes 1318928 | tf_op jit(solution)/shard_map/psum | solution.py:134
  503.5 0.8 slice.59
  504.4 1.4 fusion.17
  505.7 1.2 fusion.20
  506.9 0.4 fusion.33
  507.4 3.3 fusion.8
  510.7 4.6 copy.65
  515.3 1.8 gather_fusion.5
  517.2 1.1 fusion.12
  518.3 0.6 convolution_bitcast_fusion.4
  518.9 0.6 fusion.13
  519.5 0.7 dynamic-slice_bitcast_fusion
  520.2 0.7 add_multiply_fusion
  (54 shorter events, 1.0 us)
Async XLA Ops:
  10.1 12.0 %copy-start.4 = (bf16[512]{0:T(512)(128)(2,1)S(1)}, bf16[512]{0:T(512)(128)(2,1)}, u32[]{:S(2)}) copy-start(bf16[512]{0:T(512)(128)(2,1)} %param.10) | copy-start | bytes 3076
  10.1 12.0 %copy-start.5 = (s32[512]{0:T(512)S(1)}, s32[512]{0:T(512)}, u32[]{:S(2)}) copy-start(s32[512]{0:T(512)} %param.11) | copy-start | bytes 6148
  67.0 8.4 %copy-start.3 = (s32[256]{0:T(256)S(1)}, s32[256]{0:T(256)}, u32[]{:S(2)}) copy-start(s32[256]{0:T(256)} %param.13) | copy-start | bytes 3076
  67.0 11.6 %copy-start.2 = (bf16[512,32]{0,1:T(8,128)(2,1)S(1)}, bf16[512,32]{0,1:T(8,128)(2,1)}, u32[]{:S(2)}) copy-start(bf16[512,32]{0,1:T(8,128)(2,1)} %param.9) | copy-start | bytes 98308
  67.0 269.9 %copy-start = (s32[32768]{0:T(1024)S(1)}, s32[32768]{0:T(1024)}, u32[]{:S(2)}) copy-start(s32[32768]{0:T(1024)} %param.14) | copy-start | bytes 393220
  67.0 269.9 %copy-start.1 = (f32[32768]{0:T(1024)S(1)}, f32[32768]{0:T(1024)}, u32[]{:S(2)}) copy-start(f32[32768]{0:T(1024)} %param.12) | copy-start | bytes 393220
  67.0 301.7 %all-to-all-start = ((bf16[512,16,8,128]{3,0,2,1:T(8,128)(2,1)}), bf16[512,16,8,128]{3,0,2,1:T(8,128)(2,1)}, u32[]{:S(2)}, u32[]{:S(2)}) async-start(bf16[512,16,8,128]{3,0,2,1:T(8,128)(2,1)} %select_multiply_fusion), calls=%async_computation | async-start | bytes 33554432 | tf_op jit(solution)/shard_map/all_to_all | solution.py:126
  75.4 428.1 %all-reduce.3.cloned.1.call-start = ((), (), s32[]{:S(2)}) async-start(), calls=%async_computation.1 | async-start | bytes 2752512 | tf_op jit(solution)/shard_map/psum | solution.py:134
  434.6 85.6 %copy-start.6 = (f32[8]{0:T(128)S(1)}, f32[8]{0:T(128)}, u32[]{:S(2)}) copy-start(f32[8]{0:T(128)} %constant.200.clone) | copy-start | bytes 100
  434.6 85.6 %copy-start.7 = (f32[8]{0:T(128)S(1)}, f32[8]{0:T(128)}, u32[]{:S(2)}) copy-start(f32[8]{0:T(128)} %constant.202) | copy-start | bytes 100
Sparse Core Ops, SparseCore 0:
  434.7 68.7 all-reduce.2
